TPU v7x, 512 devices: a whole 4x8x8 slice. The times are simulated.
512 devices in a mesh: dp: 64 (over x, y, z_hi), head: 8 (over z_lo, core).
Axes of the slice: x: 4, y: 8, z: 8 (z_hi: 2, z_lo: 4; z = z_hi * 4 + z_lo), core: 2. Of those that a mesh axis runs over, the one named last changes fastest.
Arguments:
- tokens: bfloat16 [16384, 8192], P('dp', 'head'), may hold values from -6 to 6
- key_weight: bfloat16 [8192, 1024], P('dp', 'head'), may hold values from -0.0625 to 0.0625
- queries: bfloat16 [16384, 8192], P('dp', 'head'), may hold values from -51 to 51
- values: bfloat16 [16384, 1024], P('dp', 'head'), may hold values from -6 to 6
- out_grad: bfloat16 [16384, 8192], P('dp', 'head'), may hold values from -6 to 6
Outputs:
- query_grad: bfloat16 [16384, 8192], P('dp', 'head')
- value_grad: bfloat16 [16384, 1024], P('dp', 'head')
- weight_grad: float32 [8192, 1024], P('dp', 'head')
All inputs are finite; a program needn't handle non-finite values.
Results may differ from a plain program's by a relative error of at most 0.022.
The roundings to bfloat16 on the way count: a program that leaves them out, or rounds other values in their place, can miss the bound.
Values may be sent and summed in bfloat16 or wider, within the bound.
No kernel may reach another device: no remote copies, remote signals or barrier semaphores. Data moves between devices by JAX's collectives and lax.ppermute only.
A program may use at most 64 MiB of HBM per device.

v0:
```python
import jax
import jax.numpy as jnp
from jax import lax
from jax.sharding import PartitionSpec as P


def on_device(tokens, key_weight, queries, values, out_grad):
    width = values.shape[1]
    length = tokens.shape[0]
    group = queries.shape[1] // width
    scale = width ** (-0.5)
    gathered = lax.all_gather(tokens, "head", axis=1, tiled=True)
    columns = gathered
    keys = jnp.dot(
        columns,
        lax.all_gather(key_weight, "dp", axis=0, tiled=True),
        preferred_element_type=jnp.float32,
    ).astype(jnp.bfloat16)
    query_heads = queries.reshape(length, group, width)
    grad_heads = out_grad.reshape(length, group, width)
    scores = (
        jnp.einsum("qgd,kd->gqk", query_heads, keys, preferred_element_type=jnp.float32) * scale
    )
    rows = lax.broadcasted_iota(jnp.int32, (length, length), 0)
    cols = lax.broadcasted_iota(jnp.int32, (length, length), 1)
    keep = rows >= cols
    scores = jnp.where(keep, scores, jnp.float32(-1e30))
    top = jnp.max(scores, axis=-1, keepdims=True)
    expo = jnp.where(keep, jnp.exp(scores - top), jnp.float32(0.0))
    probs = expo / jnp.sum(expo, axis=-1, keepdims=True)
    weights = probs.astype(jnp.bfloat16)
    attended = jnp.einsum(
        "gqk,kd->qgd", weights, values, preferred_element_type=jnp.float32
    ).astype(jnp.bfloat16)
    dprobs = jnp.einsum("qgd,kd->gqk", grad_heads, values, preferred_element_type=jnp.float32)
    delta = jnp.transpose(
        jnp.sum(grad_heads.astype(jnp.float32) * attended.astype(jnp.float32), axis=-1), (1, 0)
    )
    dscores = (probs * (dprobs - delta[..., None])).astype(jnp.bfloat16)
    query_grad = (
        jnp.einsum("gqk,kd->qgd", dscores, keys, preferred_element_type=jnp.float32) * scale
    ).astype(jnp.bfloat16)
    key_grad = (
        jnp.einsum("gqk,qgd->kd", dscores, query_heads, preferred_element_type=jnp.float32) * scale
    ).astype(jnp.bfloat16)
    value_grad = jnp.einsum(
        "gqk,qgd->kd", weights, grad_heads, preferred_element_type=jnp.float32
    ).astype(jnp.bfloat16)
    columns = gathered
    weight_grad = lax.psum_scatter(
        lax.dot_general(
            columns, key_grad, (((0,), (0,)), ((), ())), preferred_element_type=jnp.float32
        ),
        "dp",
        scatter_dimension=0,
        tiled=True,
    )
    return (query_grad.reshape(length, group * width), value_grad, weight_grad)


def solution(mesh):
    placed = (P("dp", "head"), P("dp", "head"), P("dp", "head"), P("dp", "head"), P("dp", "head"))
    return jax.shard_map(
        on_device,
        mesh=mesh,
        in_specs=placed,
        out_specs=(P("dp", "head"), P("dp", "head"), P("dp", "head")),
        check_vma=False,
    )
```

profile of v0, /device:TPU:64, one launch (start us, length us, event | category | flops | bytes accessed | tf_op | source)
XLA Modules:
  0.0 685.2 jit_solution(2538484777238833299)
XLA Ops:
  7.2 0.0 copy-start
  7.2 0.0 all-gather.5.cloned.1.call-start
  7.2 0.7 all-gather.5.cloned.1.call-update
  7.9 0.0 all-gather.3.cloned.1.call-start
  8.0 0.7 all-gather.3.cloned.1.call-update
  8.7 0.0 reduce-scatter.2.cloned.1.call-start
  8.7 1.2 copy.9
  10.0 144.5 %all-gather.5.cloned.1.call-done = bf16[8192,128]{1,0:T(8,128)(2,1)} async-done(((bf16[128,128]{1,0:T(8,128)(2,1)}), bf16[8192,128]{1,0:T(8,128)(2,1)}) %all-gather.5.cloned.1.call-update) | async-done | bytes 2097168 | tf_op jit(solution)/shard_map/all_gather | solution.py:16
  154.5 48.9 %all-gather.3.cloned.1.call-done = bf16[256,8192]{1,0:T(8,128)(2,1)} async-done(((bf16[256,1024]{1,0:T(8,128)(2,1)}), bf16[256,8192]{1,0:T(8,128)(2,1)}) %all-gather.3.cloned.1.call-update) | async-done | bytes 4194320 | tf_op jit(solution)/shard_map/all_gather | solution.py:12
  203.5 4.1 fusion.12
  207.6 0.0 copy-done
  207.6 2.3 fusion.36
  209.8 0.0 copy-start.2
  209.8 0.0 copy-start.1
  209.8 1.9 fusion.16
  211.8 0.0 copy-done.2
  211.8 0.4 fusion.8
  212.2 0.0 copy-done.1
  212.2 0.4 fusion.2
  212.6 5.3 convolution_bitcast_fusion
  217.9 0.0 reduce-scatter.2.cloned.1.call-update
  217.9 1.1 fusion.7
  219.0 2.0 copy.16
  221.1 1.1 fusion.10
  222.1 454.9 %reduce-scatter.2.cloned.1.call-done = f32[128,128]{0,1:T(8,128)} async-done(((f32[8192,128]{0,1:T(8,128)}), f32[128,128]{0,1:T(8,128)}) %reduce-scatter.2.cloned.1.call-update) | async-done | bytes 65552 | tf_op jit(solution)/shard_map/reduce_scatter | solution.py:50
  677.1 1.6 copy.17
  (1 shorter events, 0.0 us)
Async XLA Ops:
  7.2 200.4 %copy-start = (bf16[256,1024]{1,0:T(8,128)(2,1)S(1)}, bf16[256,1024]{1,0:T(8,128)(2,1)}, u32[]{:S(2)}) copy-start(bf16[256,1024]{1,0:T(8,128)(2,1)} %param.7) | copy-start | bytes 1572868
  7.2 147.4 %all-gather.5.cloned.1.call-start = ((), (), s32[]{:S(2)}) async-start(), calls=%async_computation.2 | async-start | bytes 2129920 | tf_op jit(solution)/shard_map/all_gather | solution.py:16
  7.9 195.5 %all-gather.3.cloned.1.call-start = ((), (), s32[]{:S(2)}) async-start(), calls=%async_computation.1 | async-start | bytes 4718592 | tf_op jit(solution)/shard_map/all_gather | solution.py:12
  8.7 668.4 %reduce-scatter.2.cloned.1.call-start = ((), (), s32[]{:S(2)}) async-start(), calls=%async_computation.3 | async-start | bytes 4259840 | tf_op jit(solution)/shard_map/reduce_scatter | solution.py:50
  209.8 1.9 copy-start.2
  209.8 2.3 copy-start.1
Sparse Core Ops, SparseCore 0:
  12.5 141.9 all-gather.4
  156.6 46.7 all-gather.2
  218.1 458.9 reduce-scatter.1
where the time goes:
time: 685 us
  waiting for transfers between devices  650 us (95%)
  matrix products  14.7 us (2%)
  between operations  13.8 us (2%)
    reduce_scatter x1, waiting for transfers between devices, on_device(): lax.psum_scatter(lax.dot_general(columns, key_grad, (((0,), (0,)), ((), (...  455 us
    all_gather x1, waiting for transfers between devices, on_device(): lax.all_gather(key_weight, 'dp', axis=0, tiled=True)  145 us
    all_gather x1, waiting for transfers between devices, on_device(): gathered = lax.all_gather(tokens, 'head', axis=1, tiled=True)  48.9 us
  transfers between devices with their start and end apart: 3, of which 3 were waited for; matrix products, arithmetic and copies ran while one was open for 1% of the time, Pallas kernels for 0%

commit v1 on v0

--- a/solution.py
+++ b/solution.py
@@ -13,7 +13,9 @@
     columns = gathered
     keys = jnp.dot(
         columns,
-        lax.all_gather(key_weight, "dp", axis=0, tiled=True),
+        jnp.concatenate(
+            lax.all_to_all(jnp.stack([key_weight] * lax.axis_size("dp")), "dp", 0, 0), axis=0
+        ),
         preferred_element_type=jnp.float32,
     ).astype(jnp.bfloat16)
     query_heads = queries.reshape(length, group, width)

time: 685 us -> 592 us (0.86)
  waiting for transfers between devices: 650 us -> 536 us
  starting transfers between devices: 0.11 us -> 18.2 us
    all_gather x1 -> x0, waiting for transfers between devices: 145 us -> none  [on_device(): lax.all_gather(key_weight, 'dp', axis=0, tiled=True)]
    all_to_all x0 -> x1, waiting for transfers between devices: none -> 55.2 us  [on_device(): lax.all_to_all(jnp.stack([key_weight] * lax.axis_size('dp')), 'dp', 0, 0)]
    all_gather x1, waiting for transfers between devices: 48.9 us -> 27.5 us  [on_device(): gathered = lax.all_gather(tokens, 'head', axis=1, tiled=True)]
    all_to_all x0 -> x1, starting transfers between devices: none -> 18.1 us  [on_device(): lax.all_to_all(jnp.stack([key_weight] * lax.axis_size('dp')), 'dp', 0, 0)]
where the time goes in v1:
time: 592 us
  waiting for transfers between devices  536 us (91%)
  starting transfers between devices  18.2 us (3%)
  between operations  14.1 us (2%)
  matrix products  14 us (2%)
  local copies, waits for them, and re-layouts  7.46 us (1%)
    reduce_scatter x1, waiting for transfers between devices, on_device(): lax.psum_scatter(lax.dot_general(columns, key_grad, (((0,), (0,)), ((), (...  453 us
    all_to_all x1, waiting for transfers between devices, on_device(): lax.all_to_all(jnp.stack([key_weight] * lax.axis_size('dp')), 'dp', 0, 0)  55.2 us
    all_gather x1, waiting for transfers between devices, on_device(): gathered = lax.all_gather(tokens, 'head', axis=1, tiled=True)  27.5 us
    all_to_all x1, starting transfers between devices, on_device(): lax.all_to_all(jnp.stack([key_weight] * lax.axis_size('dp')), 'dp', 0, 0)  18.1 us
  transfers between devices with their start and end apart: 3, of which 3 were waited for; matrix products, arithmetic and copies ran while one was open for 1% of the time, Pallas kernels for 0%

profile of v1, /device:TPU:64, one launch (start us, length us, event | category | flops | bytes accessed | tf_op | source)
XLA Modules:
  0.0 592.0 jit_solution(14355670110173507590)
XLA Ops:
  7.2 0.0 copy-start
  7.2 0.0 all-gather.2.cloned.1.call-start
  7.2 0.7 all-gather.2.cloned.1.call-update
  7.9 2.6 stack.2
  10.5 18.1 %all-to-all-start = ((bf16[64,128,128]{2,1,0:T(8,128)(2,1)}), bf16[64,128,128]{2,1,0:T(8,128)(2,1)S(1)}, u32[]{:S(2)}, u32[]{:S(2)}) async-start(bf16[64,128,128]{2,1,0:T(8,128)(2,1)} %stack.2), calls=%async_computation | async-start | bytes 4194304 | tf_op jit(solution)/shard_map/all_to_all | solution.py:17
  28.6 0.0 reduce-scatter.2.cloned.1.call-start
  28.7 1.2 copy.9
  30.0 55.2 %all-to-all-done = bf16[64,128,128]{2,1,0:T(8,128)(2,1)S(1)} async-done(((bf16[64,128,128]{2,1,0:T(8,128)(2,1)}), bf16[64,128,128]{2,1,0:T(8,128)(2,1)S(1)}, u32[]{:S(2)}, u32[]{:S(2)}) %all-to-all-start) | async-done | bytes 2097184 | tf_op jit(solution)/shard_map/all_to_all | solution.py:17
  85.1 27.5 %all-gather.2.cloned.1.call-done = bf16[256,8192]{1,0:T(8,128)(2,1)} async-done(((bf16[256,1024]{1,0:T(8,128)(2,1)}), bf16[256,8192]{1,0:T(8,128)(2,1)}) %all-gather.2.cloned.1.call-update) | async-done | bytes 4194320 | tf_op jit(solution)/shard_map/all_gather | solution.py:12
  112.6 3.4 fusion.12
  116.1 0.0 copy-done
  116.1 2.3 fusion.36
  118.4 0.0 copy-start.2
  118.4 0.0 copy-start.1
  118.4 1.9 fusion.16
  120.3 0.0 copy-done.2
  120.3 0.4 fusion.8
  120.7 0.0 copy-done.1
  120.7 0.4 fusion.2
  121.1 5.3 convolution_bitcast_fusion
  126.4 0.0 reduce-scatter.2.cloned.1.call-update
  126.5 1.1 fusion.7
  127.6 2.0 copy.16
  129.6 1.1 fusion.10
  130.7 452.9 %reduce-scatter.2.cloned.1.call-done = f32[128,128]{0,1:T(8,128)} async-done(((f32[8192,128]{0,1:T(8,128)}), f32[128,128]{0,1:T(8,128)}) %reduce-scatter.2.cloned.1.call-update) | async-done | bytes 65552 | tf_op jit(solution)/shard_map/reduce_scatter | solution.py:52
  583.6 1.6 copy.17
  (1 shorter events, 0.0 us)
Async XLA Ops:
  7.2 108.9 %copy-start = (bf16[256,1024]{1,0:T(8,128)(2,1)S(1)}, bf16[256,1024]{1,0:T(8,128)(2,1)}, u32[]{:S(2)}) copy-start(bf16[256,1024]{1,0:T(8,128)(2,1)} %param.7) | copy-start | bytes 1572868
  7.2 105.5 %all-gather.2.cloned.1.call-start = ((), (), s32[]{:S(2)}) async-start(), calls=%async_computation.2 | async-start | bytes 4718592 | tf_op jit(solution)/shard_map/all_gather | solution.py:12
  10.5 74.6 %all-to-all-start = ((bf16[64,128,128]{2,1,0:T(8,128)(2,1)}), bf16[64,128,128]{2,1,0:T(8,128)(2,1)S(1)}, u32[]{:S(2)}, u32[]{:S(2)}) async-start(bf16[64,128,128]{2,1,0:T(8,128)(2,1)} %stack.2), calls=%async_computation | async-start | bytes 4194304 | tf_op jit(solution)/shard_map/all_to_all | solution.py:17
  28.6 554.9 %reduce-scatter.2.cloned.1.call-start = ((), (), s32[]{:S(2)}) async-start(), calls=%async_computation.3 | async-start | bytes 4259840 | tf_op jit(solution)/shard_map/reduce_scatter | solution.py:52
  118.4 1.9 copy-start.2
  118.4 2.3 copy-start.1
Sparse Core Ops, SparseCore 0:
  10.1 102.5 all-gather.1
  126.6 456.9 reduce-scatter.1
